TPU v7x, 32 devices: a whole 2x2x4 slice. The times are simulated.
32 devices in a mesh: ctx: 4 (over y, x), head: 8 (over z, core).
Axes of the slice: x: 2, y: 2, z: 4, core: 2. Of those that a mesh axis runs over, the one named last changes fastest.
Arguments:
- query_rows: bfloat16 [4096, 8192], P('ctx', 'head'), may hold values from -6 to 6
- key_rows: bfloat16 [4096, 8192], P('ctx', 'head'), may hold values from -6 to 6
- value_rows: bfloat16 [4096, 8192], P('ctx', 'head'), may hold values from -6 to 6
- decay_rate: float32 [64], P('head'), as said below
- starts: int32 [4096], P('ctx'), may hold values 0 or 1
- norm_gain: float32 [8192], P('head'), may hold values from 0.1 to 1.9
- grad_out: bfloat16 [4096, 8192], P('ctx', 'head'), may hold values from -6 to 6
Outputs:
- normed: bfloat16 [4096, 8192], P('ctx', 'head')
- grad_query: bfloat16 [4096, 8192], P('ctx', 'head')
- grad_key: bfloat16 [4096, 8192], P('ctx', 'head')
- grad_value: bfloat16 [4096, 8192], P('ctx', 'head')
Inputs may be any that keep to these rules, and one draw needn't show every extreme that they name: `decay_rate`: positive rates; a head keeps exp(-rate) of its state per position. `starts`: 1 where a document begins, 0 elsewhere.
All inputs are finite; a program needn't handle non-finite values. No bound on the sum of `starts` on one device may be relied on, other than what follows from the above.
Results may differ from a plain program's by a relative error of at most 0.008.
Values sent between devices are 32-bit elements; how exact they have to be, the bound alone decides.
A program may use at most 128 MiB of HBM per device.

v0:
```python
import functools

import jax
import jax.numpy as jnp
from jax import lax
from jax.experimental import pallas as pl
from jax.experimental.pallas import tpu as pltpu
from jax.sharding import PartitionSpec as P

HEADS = 64
DH = 128
CHUNK = 256
EPSILON = 1e-06
MESH = pl.DeviceIdType.MESH
F32 = jnp.float32
BF16 = jnp.bfloat16


def dot(a, b, da, db):
    return lax.dot_general(a, b, (((da,), (db,)), ((), ())), preferred_element_type=F32)


def kernel(
    steps, peers, total,
    q_hbm, k_hbm, v_hbm, g_hbm, rate_ref, starts_ref, gain_ref,
    n_out, gq_out, gk_out, gv_out,
    qs, ks, vs, gs, att, ga, weights, gkp, gvp, ns, gqs, gks, gvs,
    joined, in_mask, out_mask, clear, d_state, full_state, d_grad,
    own, got, pre, sq_acc, cr_acc, inv_full, coef_full, x_buf,
    in_sem, out_sem, s_send, s_recv, x_send, x_recv,
):
    heads, rows, _ = qs.shape
    chunks = rows // CHUNK
    ctx = lax.axis_index("ctx")
    me = lax.axis_index("head")

    def cols(h):
        return pl.ds(pl.multiple_of(h * DH, DH), DH)

    def load(i, h):
        hbm, buf = ((k_hbm, ks), (v_hbm, vs), (q_hbm, qs), (g_hbm, gs))[i]
        return pltpu.make_async_copy(hbm.at[:, cols(h)], buf.at[h], in_sem.at[i, h])

    def store(i, h):
        buf, hbm = ((ns, n_out), (gqs, gq_out), (gks, gk_out), (gvs, gv_out))[i]
        return pltpu.make_async_copy(buf.at[h], hbm.at[:, cols(h)], out_sem.at[i, h])

    def partner(step):
        size = 1 << step
        bit = (ctx // size) % 2
        return bit, ctx + size - 2 * size * bit

    def scan_copy(which, step, h):
        return pltpu.make_async_remote_copy(
            src_ref=own.at[which, step, h],
            dst_ref=got.at[which, step, h],
            send_sem=s_send.at[which, step, h],
            recv_sem=s_recv.at[which, step, h],
            device_id=(partner(step)[1], me),
            device_id_type=MESH,
        )

    def swap_copy(k):
        return pltpu.make_async_remote_copy(
            src_ref=x_buf.at[0],
            dst_ref=x_buf.at[k],
            send_sem=x_send.at[k],
            recv_sem=x_recv.at[k],
            device_id=(ctx, (me + k) % peers),
            device_id_type=MESH,
        )

    def start_loads(pair):
        def go(h, c):
            for i in pair:
                load(i, h).start()
            return c
        lax.fori_loop(0, heads, go, 0)

    start_loads((0, 1))
    start_loads((2, 3))

    barrier = pltpu.get_barrier_semaphore()
    for step in range(steps):
        pl.semaphore_signal(barrier, inc=1, device_id=(partner(step)[1], me), device_id_type=MESH)

    def greet(k, c):
        pl.semaphore_signal(
            barrier, inc=1, device_id=(ctx, (me + k) % peers), device_id_type=MESH
        )
        return c

    lax.fori_loop(1, peers, greet, 0)

    row_at = lax.broadcasted_iota(jnp.int32, (CHUNK, CHUNK), 0)
    col_at = lax.broadcasted_iota(jnp.int32, (CHUNK, CHUNK), 1)
    lower = row_at >= col_at
    ones_low = jnp.where(lower, 1.0, 0.0).astype(BF16)
    for c in range(chunks):
        flags = starts_ref[:, c * CHUNK:(c + 1) * CHUNK].astype(F32)
        wide = jnp.broadcast_to(flags, (DH, CHUNK)).astype(BF16)
        run_row = dot(wide, ones_low, 1, 1)[0:1, :]
        run_col = dot(ones_low, wide, 1, 1)
        count = jnp.sum(flags, axis=1, keepdims=True)
        both = jnp.concatenate([run_col] * (CHUNK // DH), axis=1)
        joined[c] = jnp.where(lower & (both == run_row), 1.0, 0.0)
        in_mask[c] = jnp.where(run_col == 0.0, 1.0, 0.0)
        out_mask[c] = jnp.where(run_col == count, 1.0, 0.0)
        clear[c] = jnp.broadcast_to(jnp.where(count == 0.0, 1.0, 0.0), (8, DH))
    sq_acc[...] = jnp.zeros_like(sq_acc)
    cr_acc[...] = jnp.zeros_like(cr_acc)

    place = lax.broadcasted_iota(jnp.int32, (CHUNK, DH), 0).astype(F32)
    gap = jnp.maximum(row_at - col_at, 0).astype(F32)

    def reach_in(rate):
        return jnp.exp(-rate * (place + 1.0))

    def reach_out(rate):
        return jnp.exp(-rate * (CHUNK - 1.0 - place))

    def carry(rate, c):
        return clear[c] * jnp.exp(jnp.full((8, DH), -rate * CHUNK, F32))

    def put(which, step, h, state, factor):
        own[which, step, h, 0:DH, :] = state
        own[which, step, h, DH:DH + 8, :] = factor

    def take(which, step, h, want_total):
        scan_copy(which, step, h).wait_recv()
        bit, _ = partner(step)
        ahead = (bit == 1) if which == 0 else (bit == 0)
        came, came_f = got[which, step, h, 0:DH, :], got[which, step, h, DH:DH + 8, :]
        if step == 0:
            state = jnp.where(ahead, came, 0.0)
            factor = jnp.where(ahead, came_f, 1.0)
        else:
            old, old_f = pre[h, 0:DH, :], pre[h, DH:DH + 8, :]
            state = jnp.where(ahead, old_f[0:1, :] * came + old, old)
            factor = jnp.where(ahead, old_f * came_f, old_f)
        if not want_total:
            return state
        pre[h, 0:DH, :] = state
        pre[h, DH:DH + 8, :] = factor
        mine, mine_f = own[which, step, h, 0:DH, :], own[which, step, h, DH:DH + 8, :]
        merged = jnp.where(ahead, mine_f[0:1, :] * came + mine, came_f[0:1, :] * mine + came)
        put(which, step + 1, h, merged, mine_f * came_f)
        scan_copy(which, step + 1, h).start()
        return None

    def part(c):
        return slice(c * CHUNK, (c + 1) * CHUNK)

    pl.semaphore_wait(barrier, steps + peers - 1)

    def make_states(h, carried):
        load(0, h).wait()
        load(1, h).wait()
        rate = rate_ref[h]
        out = reach_out(rate)
        state = jnp.zeros((DH, DH), F32)
        factor = jnp.ones((8, DH), F32)
        for c in range(chunks):
            weighted = (ks[h, part(c), :].astype(F32) * (out * out_mask[c])).astype(BF16)
            add = dot(weighted, vs[h, part(c), :], 0, 0)
            d_state[h, c] = add
            keep = carry(rate, c)
            state = keep[0:1, :] * state + add
            factor = factor * keep
        put(0, 0, h, state, factor)
        scan_copy(0, 0, h).start()
        return carried

    lax.fori_loop(0, heads, make_states, 0)

    def attend(h, carried):
        load(2, h).wait()
        load(3, h).wait()
        decay = jnp.exp(-rate_ref[h] * gap)
        for c in range(chunks):
            scores = dot(qs[h, part(c), :], ks[h, part(c), :], 1, 1)
            w = (scores * (decay * joined[c])).astype(BF16)
            weights[h, c] = w
            att[h, part(c), :] = dot(w, vs[h, part(c), :], 1, 0)
        for step in range(steps - 1):
            take(0, step, h, True)
        return carried

    lax.fori_loop(0, heads, attend, 0)

    def finish_attend(h, carried):
        rate = rate_ref[h]
        state = take(0, steps - 1, h, False)
        reach = reach_in(rate)
        gain = gain_ref[pl.ds(h, 1), :]
        for c in range(chunks):
            small = state.astype(BF16)
            full_state[h, c] = small
            a = att[h, part(c), :] + (reach * in_mask[c]) * dot(qs[h, part(c), :], small, 1, 0)
            att[h, part(c), :] = a
            sq_acc[part(c), :] += a * a
            cr_acc[part(c), :] += gs[h, part(c), :].astype(F32) * gain * a
            if c < chunks - 1:
                state = carry(rate, c)[0:1, :] * state + d_state[h, c]
        return carried

    lax.fori_loop(0, heads, finish_attend, 0)

    x_buf[0, 0:1, :] = jnp.sum(jnp.transpose(sq_acc[...]), axis=0, keepdims=True)
    x_buf[0, 1:2, :] = jnp.sum(jnp.transpose(cr_acc[...]), axis=0, keepdims=True)

    def send(k, c):
        swap_copy(k).start()
        return c

    lax.fori_loop(1, peers, send, 0)

    def receive(k, c):
        swap_copy(k).wait_recv()
        return c + x_buf[k]

    sums = lax.fori_loop(1, peers, receive, x_buf[0])
    inverse = 1.0 / jnp.sqrt(sums[0:1, :] / total + EPSILON)
    coef = inverse * inverse * inverse * (sums[1:2, :] / total)
    inv_full[...] = jnp.transpose(jnp.broadcast_to(inverse, (DH, rows)))
    coef_full[...] = jnp.transpose(jnp.broadcast_to(coef, (DH, rows)))

    def make_grads(h, carried):
        rate = rate_ref[h]
        reach = reach_in(rate)
        gain = gain_ref[pl.ds(h, 1), :]
        state = jnp.zeros((DH, DH), F32)
        factor = jnp.ones((8, DH), F32)
        for c in reversed(range(chunks)):
            a, inv = att[h, part(c), :], inv_full[part(c), :]
            ns[h, part(c), :] = (a * inv * gain).astype(BF16)
            gained = gs[h, part(c), :].astype(F32) * gain
            grad = (inv * gained - a * coef_full[part(c), :]).astype(BF16)
            ga[h, part(c), :] = grad
            weighted = (qs[h, part(c), :].astype(F32) * (reach * in_mask[c])).astype(BF16)
            add = dot(weighted, grad, 0, 0)
            d_grad[h, c] = add
            keep = carry(rate, c)
            state = keep[0:1, :] * state + add
            factor = factor * keep
        put(1, 0, h, state, factor)
        scan_copy(1, 0, h).start()
        store(0, h).start()
        return carried

    lax.fori_loop(0, heads, make_grads, 0)

    def inner_grads(h, carried):
        rate = rate_ref[h]
        decay = jnp.exp(-rate * gap)
        reach = reach_in(rate)
        for c in range(chunks):
            grad = ga[h, part(c), :]
            d = (dot(grad, vs[h, part(c), :], 1, 1) * (decay * joined[c])).astype(BF16)
            gq = dot(d, ks[h, part(c), :], 1, 0)
            gq += (reach * in_mask[c]) * dot(grad, full_state[h, c], 1, 1)
            gqs[h, part(c), :] = gq.astype(BF16)
            gkp[h, part(c), :] = dot(d, qs[h, part(c), :], 0, 0)
            gvp[h, part(c), :] = dot(weights[h, c], grad, 0, 0)
        for step in range(steps - 1):
            take(1, step, h, True)
        store(1, h).start()
        return carried

    lax.fori_loop(0, heads, inner_grads, 0)

    def finish_grads(h, carried):
        rate = rate_ref[h]
        state = take(1, steps - 1, h, False)
        out = reach_out(rate)
        for c in reversed(range(chunks)):
            small = state.astype(BF16)
            reach = out * out_mask[c]
            gk = gkp[h, part(c), :] + reach * dot(vs[h, part(c), :], small, 1, 1)
            gv = gvp[h, part(c), :] + reach * dot(ks[h, part(c), :], small, 1, 0)
            gks[h, part(c), :] = gk.astype(BF16)
            gvs[h, part(c), :] = gv.astype(BF16)
            if c > 0:
                state = carry(rate, c)[0:1, :] * state + d_grad[h, c]
        store(2, h).start()
        store(3, h).start()
        return carried

    lax.fori_loop(0, heads, finish_grads, 0)

    def drain(h, carried):
        for which in range(2):
            for step in range(steps):
                scan_copy(which, step, h).wait_send()
        for i in range(4):
            store(i, h).wait()
        return carried

    lax.fori_loop(0, heads, drain, 0)

    def drain_swaps(k, c):
        swap_copy(k).wait_send()
        return c

    lax.fori_loop(1, peers, drain_swaps, 0)


def body(steps, peers, query_rows, key_rows, value_rows, decay_rate, starts, norm_gain, grad_out):
    rows, features = query_rows.shape
    heads = features // DH
    chunks = rows // CHUNK
    big = jax.ShapeDtypeStruct((rows, features), BF16)
    whole = pl.BlockSpec(memory_space=pl.ANY)
    inside = pl.BlockSpec(memory_space=pltpu.VMEM)

    def head_rows(dtype):
        return pltpu.VMEM((heads, rows, DH), dtype)

    dma = pltpu.SemaphoreType.DMA
    return pl.pallas_call(
        functools.partial(kernel, steps, peers, HEADS * DH),
        out_shape=(big,) * 4,
        in_specs=[whole] * 4 + [pl.BlockSpec(memory_space=pltpu.SMEM), inside, inside],
        out_specs=(whole,) * 4,
        scratch_shapes=[head_rows(BF16)] * 4
        + [head_rows(F32), head_rows(BF16), pltpu.VMEM((heads, chunks, CHUNK, CHUNK), BF16)]
        + [head_rows(F32)] * 2
        + [head_rows(BF16)] * 4
        + [
            pltpu.VMEM((chunks, CHUNK, CHUNK), F32),
            pltpu.VMEM((chunks, CHUNK, DH), F32),
            pltpu.VMEM((chunks, CHUNK, DH), F32),
            pltpu.VMEM((chunks, 8, DH), F32),
            pltpu.VMEM((heads, chunks, DH, DH), F32),
            pltpu.VMEM((heads, chunks, DH, DH), BF16),
            pltpu.VMEM((heads, chunks, DH, DH), F32),
            pltpu.VMEM((2, steps, heads, DH + 8, DH), F32),
            pltpu.VMEM((2, steps, heads, DH + 8, DH), F32),
            pltpu.VMEM((heads, DH + 8, DH), F32),
            pltpu.VMEM((rows, DH), F32),
            pltpu.VMEM((rows, DH), F32),
            pltpu.VMEM((rows, DH), F32),
            pltpu.VMEM((rows, DH), F32),
            pltpu.VMEM((peers, 2, rows), F32),
            dma((4, heads)),
            dma((4, heads)),
            dma((2, steps, heads)),
            dma((2, steps, heads)),
            dma((peers,)),
            dma((peers,)),
        ],
        compiler_params=pltpu.CompilerParams(
            collective_id=0, has_side_effects=True, vmem_limit_bytes=60 * 1024 * 1024
        ),
    )(
        query_rows, key_rows, value_rows, grad_out, decay_rate,
        starts.reshape(1, rows), norm_gain.reshape(heads, DH),
    )


def solution(mesh):
    steps = (mesh.shape["ctx"] - 1).bit_length()
    both = P("ctx", "head")
    return jax.shard_map(
        functools.partial(body, steps, mesh.shape["head"]),
        mesh=mesh,
        in_specs=(both, both, both, P("head"), P("ctx"), P("head"), both),
        out_specs=(both,) * 4,
        check_vma=False,
    )
```

profile of v0, /device:TPU:0, one launch (start us, length us, event | category | flops | bytes accessed | tf_op | source)
XLA Modules:
  0.0 58.6 jit_solution(5199433748590574633)
XLA Ops:
  0.6 48.7 %shard_map.102 = (bf16[1024,1024]{1,0:T(8,128)(2,1)}, bf16[1024,1024]{1,0:T(8,128)(2,1)}, bf16[1024,1024]{1,0:T(8,128)(2,1)}, bf16[1024,1024]{1,0:T(8,128)(2,1)}) custom-call(bf16[1024,1024]{1,0:T(8,128)(2,1)} %q_hbm.1, bf16[1024,1024]{1,0:T(8,128)(2,1)} %k_hbm.1, bf16[1024,1024]{1,0:T(8,128)(2,1)} %v_hbm.1, bf16[1024,1024]{1,0:T(8,128)(2,1)} %g_hbm.1, ...), custom_call_target="tpu_custom_call" | custom-call | tf_op jit(solution)/shard_map/pallas_call | solution.py:320
  49.4 0.0 copy-start.2
  49.4 3.2 %copy.15 = bf16[1024,1024]{1,0:T(8,128)(2,1)} copy(bf16[1024,1024]{1,0:T(8,128)(2,1)} %get-tuple-element.8) | data formatting | bytes 4194304
  52.6 0.0 copy-done.2
  52.6 0.0 copy-start.1
  52.6 1.3 %copy.16 = bf16[1024,1024]{1,0:T(8,128)(2,1)} copy(bf16[1024,1024]{1,0:T(8,128)(2,1)S(1)} %copy-done.2) | data formatting | bytes 4194304
  53.9 1.0 %copy-done.1 = bf16[1024,1024]{1,0:T(8,128)(2,1)S(1)} copy-done((bf16[1024,1024]{1,0:T(8,128)(2,1)S(1)}, bf16[1024,1024]{1,0:T(8,128)(2,1)}, u32[]{:S(2)}) %copy-start.1) | copy-done | bytes 2097176
  55.0 0.0 copy-start
  55.0 1.3 %copy.17 = bf16[1024,1024]{1,0:T(8,128)(2,1)} copy(bf16[1024,1024]{1,0:T(8,128)(2,1)S(1)} %copy-done.1) | data formatting | bytes 4194304
  56.3 1.0 %copy-done = bf16[1024,1024]{1,0:T(8,128)(2,1)S(1)} copy-done((bf16[1024,1024]{1,0:T(8,128)(2,1)S(1)}, bf16[1024,1024]{1,0:T(8,128)(2,1)}, u32[]{:S(2)}) %copy-start) | copy-done | bytes 2097176
  57.3 1.3 %copy.18 = bf16[1024,1024]{1,0:T(8,128)(2,1)} copy(bf16[1024,1024]{1,0:T(8,128)(2,1)S(1)} %copy-done) | data formatting | bytes 4194304
Async XLA Ops:
  49.4 3.2 %copy-start.2 = (bf16[1024,1024]{1,0:T(8,128)(2,1)S(1)}, bf16[1024,1024]{1,0:T(8,128)(2,1)}, u32[]{:S(2)}) copy-start(bf16[1024,1024]{1,0:T(8,128)(2,1)} %get-tuple-element.9) | copy-start | bytes 6291460
  52.6 2.3 %copy-start.1 = (bf16[1024,1024]{1,0:T(8,128)(2,1)S(1)}, bf16[1024,1024]{1,0:T(8,128)(2,1)}, u32[]{:S(2)}) copy-start(bf16[1024,1024]{1,0:T(8,128)(2,1)} %get-tuple-element.10) | copy-start | bytes 6291460
  55.0 2.3 %copy-start = (bf16[1024,1024]{1,0:T(8,128)(2,1)S(1)}, bf16[1024,1024]{1,0:T(8,128)(2,1)}, u32[]{:S(2)}) copy-start(bf16[1024,1024]{1,0:T(8,128)(2,1)} %get-tuple-element.11) | copy-start | bytes 6291460
where the time goes:
time: 58.9 us; the launch traced here: 58.6 us
  Pallas kernels  48.7 us (83%)
  local copies, waits for them, and re-layouts  9.25 us (16%)
  between operations  0.65 us (1%)
    pallas_call x1, Pallas kernels, body(): pl.pallas_call(functools.partial(kernel, steps, peers, HEADS * DH), out_s...  48.7 us
    unnamed x10, local copies, waits for them, and re-layouts  9.25 us

commit v1 on v0

--- a/solution.py
+++ b/solution.py
@@ -24,10 +24,10 @@
     steps, peers, total,
     q_hbm, k_hbm, v_hbm, g_hbm, rate_ref, starts_ref, gain_ref,
     n_out, gq_out, gk_out, gv_out,
-    qs, ks, vs, gs, att, ga, weights, gkp, gvp, ns, gqs, gks, gvs,
+    qs, ks, vs, gs, att, ga, weights, gkp, gvp,
     joined, in_mask, out_mask, clear, d_state, full_state, d_grad,
     own, got, pre, sq_acc, cr_acc, inv_full, coef_full, x_buf,
-    in_sem, out_sem, s_send, s_recv, x_send, x_recv,
+    in_sem, s_send, s_recv, x_send, x_recv,
 ):
     heads, rows, _ = qs.shape
     chunks = rows // CHUNK
@@ -40,10 +40,6 @@
     def load(i, h):
         hbm, buf = ((k_hbm, ks), (v_hbm, vs), (q_hbm, qs), (g_hbm, gs))[i]
         return pltpu.make_async_copy(hbm.at[:, cols(h)], buf.at[h], in_sem.at[i, h])
-
-    def store(i, h):
-        buf, hbm = ((ns, n_out), (gqs, gq_out), (gks, gk_out), (gvs, gv_out))[i]
-        return pltpu.make_async_copy(buf.at[h], hbm.at[:, cols(h)], out_sem.at[i, h])
 
     def partner(step):
         size = 1 << step
@@ -233,7 +229,7 @@
         factor = jnp.ones((8, DH), F32)
         for c in reversed(range(chunks)):
             a, inv = att[h, part(c), :], inv_full[part(c), :]
-            ns[h, part(c), :] = (a * inv * gain).astype(BF16)
+            n_out[part(c), cols(h)] = (a * inv * gain).astype(BF16)
             gained = gs[h, part(c), :].astype(F32) * gain
             grad = (inv * gained - a * coef_full[part(c), :]).astype(BF16)
             ga[h, part(c), :] = grad
@@ -245,7 +241,6 @@
             factor = factor * keep
         put(1, 0, h, state, factor)
         scan_copy(1, 0, h).start()
-        store(0, h).start()
         return carried
 
     lax.fori_loop(0, heads, make_grads, 0)
@@ -259,12 +254,11 @@
             d = (dot(grad, vs[h, part(c), :], 1, 1) * (decay * joined[c])).astype(BF16)
             gq = dot(d, ks[h, part(c), :], 1, 0)
             gq += (reach * in_mask[c]) * dot(grad, full_state[h, c], 1, 1)
-            gqs[h, part(c), :] = gq.astype(BF16)
+            gq_out[part(c), cols(h)] = gq.astype(BF16)
             gkp[h, part(c), :] = dot(d, qs[h, part(c), :], 0, 0)
             gvp[h, part(c), :] = dot(weights[h, c], grad, 0, 0)
         for step in range(steps - 1):
             take(1, step, h, True)
-        store(1, h).start()
         return carried
 
     lax.fori_loop(0, heads, inner_grads, 0)
@@ -278,12 +272,10 @@
             reach = out * out_mask[c]
             gk = gkp[h, part(c), :] + reach * dot(vs[h, part(c), :], small, 1, 1)
             gv = gvp[h, part(c), :] + reach * dot(ks[h, part(c), :], small, 1, 0)
-            gks[h, part(c), :] = gk.astype(BF16)
-            gvs[h, part(c), :] = gv.astype(BF16)
+            gk_out[part(c), cols(h)] = gk.astype(BF16)
+            gv_out[part(c), cols(h)] = gv.astype(BF16)
             if c > 0:
                 state = carry(rate, c)[0:1, :] * state + d_grad[h, c]
-        store(2, h).start()
-        store(3, h).start()
         return carried
 
     lax.fori_loop(0, heads, finish_grads, 0)
@@ -292,8 +284,6 @@
         for which in range(2):
             for step in range(steps):
                 scan_copy(which, step, h).wait_send()
-        for i in range(4):
-            store(i, h).wait()
         return carried
 
     lax.fori_loop(0, heads, drain, 0)
@@ -303,6 +293,15 @@
         return c
 
     lax.fori_loop(1, peers, drain_swaps, 0)
+
+
+def write_out(*refs):
+    sems = refs[8]
+    copies = [pltpu.make_async_copy(refs[i], refs[i + 4], sems.at[i]) for i in range(4)]
+    for copy in copies:
+        copy.start()
+    for copy in copies:
+        copy.wait()
 
 
 def body(steps, peers, query_rows, key_rows, value_rows, decay_rate, starts, norm_gain, grad_out):
@@ -310,22 +309,21 @@
     heads = features // DH
     chunks = rows // CHUNK
     big = jax.ShapeDtypeStruct((rows, features), BF16)
-    whole = pl.BlockSpec(memory_space=pl.ANY)
+    whole = pl.BlockSpec(memory_space=pltpu.HBM)
     inside = pl.BlockSpec(memory_space=pltpu.VMEM)
 
     def head_rows(dtype):
         return pltpu.VMEM((heads, rows, DH), dtype)
 
     dma = pltpu.SemaphoreType.DMA
-    return pl.pallas_call(
+    kept = pl.pallas_call(
         functools.partial(kernel, steps, peers, HEADS * DH),
-        out_shape=(big,) * 4,
+        out_shape=(pltpu.VMEM((rows, features), BF16),) * 4,
         in_specs=[whole] * 4 + [pl.BlockSpec(memory_space=pltpu.SMEM), inside, inside],
-        out_specs=(whole,) * 4,
+        out_specs=(inside,) * 4,
         scratch_shapes=[head_rows(BF16)] * 4
         + [head_rows(F32), head_rows(BF16), pltpu.VMEM((heads, chunks, CHUNK, CHUNK), BF16)]
         + [head_rows(F32)] * 2
-        + [head_rows(BF16)] * 4
         + [
             pltpu.VMEM((chunks, CHUNK, CHUNK), F32),
             pltpu.VMEM((chunks, CHUNK, DH), F32),
@@ -343,19 +341,26 @@
             pltpu.VMEM((rows, DH), F32),
             pltpu.VMEM((peers, 2, rows), F32),
             dma((4, heads)),
-            dma((4, heads)),
             dma((2, steps, heads)),
             dma((2, steps, heads)),
             dma((peers,)),
             dma((peers,)),
         ],
         compiler_params=pltpu.CompilerParams(
-            collective_id=0, has_side_effects=True, vmem_limit_bytes=60 * 1024 * 1024
+            collective_id=0, has_side_effects=True, vmem_limit_bytes=55 * 1024 * 1024
         ),
     )(
         query_rows, key_rows, value_rows, grad_out, decay_rate,
         starts.reshape(1, rows), norm_gain.reshape(heads, DH),
     )
+    return pl.pallas_call(
+        write_out,
+        out_shape=(big,) * 4,
+        in_specs=[pl.BlockSpec(memory_space=pl.ANY)] * 4,
+        out_specs=(whole,) * 4,
+        scratch_shapes=[dma((4,))],
+        compiler_params=pltpu.CompilerParams(vmem_limit_bytes=1024 * 1024),
+    )(*kept)
 
 
 def solution(mesh):

time: 58.9 us -> 52 us (0.88)
  local copies, waits for them, and re-layouts: 9.25 us -> 0 us
  Pallas kernels: 48.7 us -> 51.2 us
    unnamed x10 -> x0, local copies, waits for them, and re-layouts: 9.25 us -> none
    pallas_call x0 -> x1, Pallas kernels: none -> 3.37 us  [body(): pl.pallas_call(write_out, out_shape=(big,) * 4, in_specs=[pl.BlockSpec(me...]
    pallas_call x1, Pallas kernels: 48.7 us -> 47.8 us  [body(): pl.pallas_call(functools.partial(kernel, steps, peers, HEADS * DH), out_s...]
where the time goes in v1:
time: 52 us; the launch traced here: 51.8 us
  Pallas kernels  51.2 us (98%)
  between operations  0.64 us (1%)
    pallas_call x1, Pallas kernels, body(): pl.pallas_call(functools.partial(kernel, steps, peers, HEADS * DH), out_s...  47.8 us
    pallas_call x1, Pallas kernels, body(): pl.pallas_call(write_out, out_shape=(big,) * 4, in_specs=[pl.BlockSpec(me...  3.37 us

profile of v1, /device:TPU:0, one launch (start us, length us, event | category | flops | bytes accessed | tf_op | source)
XLA Modules:
  0.0 51.8 jit_solution(9587876928924237471)
XLA Ops:
  0.6 47.8 %shard_map.102 = (bf16[1024,1024]{1,0:T(8,128)(2,1)S(1)}, bf16[1024,1024]{1,0:T(8,128)(2,1)S(1)}, bf16[1024,1024]{1,0:T(8,128)(2,1)S(1)}, bf16[1024,1024]{1,0:T(8,128)(2,1)S(1)}) custom-call(bf16[1024,1024]{1,0:T(8,128)(2,1)} %q_hbm.1, bf16[1024,1024]{1,0:T(8,128)(2,1)} %k_hbm.1, bf16[1024,1024]{1,0:T(8,128)(2,1)} %v_hbm.1, bf16[1024,1024]{1,0:T(8,128)(2,1)} %g_hbm.1, ...), custom_call_target="tpu_custom_call" | custom-call | tf_op jit(solution)/shard_map/pallas_call | solution.py:319
  48.5 3.4 %shard_map.103 = (bf16[1024,1024]{1,0:T(8,128)(2,1)}, bf16[1024,1024]{1,0:T(8,128)(2,1)}, bf16[1024,1024]{1,0:T(8,128)(2,1)}, bf16[1024,1024]{1,0:T(8,128)(2,1)}) custom-call(bf16[1024,1024]{1,0:T(8,128)(2,1)S(1)} %get-tuple-element.8.refs_0_, bf16[1024,1024]{1,0:T(8,128)(2,1)S(1)} %get-tuple-element.9.refs_1_, ...), custom_call_target="tpu_custom_call" | custom-call | tf_op jit(solution)/shard_map/pallas_call | solution.py:356

commit v2 on v1

--- a/solution.py
+++ b/solution.py
@@ -9,7 +9,9 @@
 
 HEADS = 64
 DH = 128
-CHUNK = 256
+CHUNK = 128
+AHEAD = 2
+AHEAD_GRADS = 3
 EPSILON = 1e-06
 MESH = pl.DeviceIdType.MESH
 F32 = jnp.float32
@@ -173,10 +175,16 @@
         load(2, h).wait()
         load(3, h).wait()
         decay = jnp.exp(-rate_ref[h] * gap)
+        def raw(c):
+            return dot(qs[h, part(c), :], ks[h, part(c), :], 1, 1)
+
+        ready = [raw(c) for c in range(min(AHEAD, chunks))]
         for c in range(chunks):
-            scores = dot(qs[h, part(c), :], ks[h, part(c), :], 1, 1)
+            scores = ready.pop(0)
+            if c + AHEAD < chunks:
+                ready.append(raw(c + AHEAD))
             w = (scores * (decay * joined[c])).astype(BF16)
-            weights[h, c] = w
+            weights[h, c] = jnp.transpose(w)
             att[h, part(c), :] = dot(w, vs[h, part(c), :], 1, 0)
         for step in range(steps - 1):
             take(0, step, h, True)
@@ -249,14 +257,20 @@
         rate = rate_ref[h]
         decay = jnp.exp(-rate * gap)
         reach = reach_in(rate)
+        def raw(c):
+            grad = ga[h, part(c), :]
+            return dot(grad, vs[h, part(c), :], 1, 1), dot(grad, full_state[h, c], 1, 1)
+
+        ready = [raw(c) for c in range(min(AHEAD_GRADS, chunks))]
         for c in range(chunks):
-            grad = ga[h, part(c), :]
-            d = (dot(grad, vs[h, part(c), :], 1, 1) * (decay * joined[c])).astype(BF16)
-            gq = dot(d, ks[h, part(c), :], 1, 0)
-            gq += (reach * in_mask[c]) * dot(grad, full_state[h, c], 1, 1)
+            wide, far = ready.pop(0)
+            if c + AHEAD_GRADS < chunks:
+                ready.append(raw(c + AHEAD_GRADS))
+            gvp[h, part(c), :] = dot(weights[h, c], ga[h, part(c), :], 1, 0)
+            d = (wide * (decay * joined[c])).astype(BF16)
+            gq = dot(d, ks[h, part(c), :], 1, 0) + (reach * in_mask[c]) * far
             gq_out[part(c), cols(h)] = gq.astype(BF16)
             gkp[h, part(c), :] = dot(d, qs[h, part(c), :], 0, 0)
-            gvp[h, part(c), :] = dot(weights[h, c], grad, 0, 0)
         for step in range(steps - 1):
             take(1, step, h, True)
         return carried

time: 52 us -> 51.5 us (level)
  no operation moved by 1% of the time
where the time goes in v2:
time: 51.5 us; the launch traced here: 51.3 us
  Pallas kernels  50.7 us (98%)
  between operations  0.64 us (1%)
    pallas_call x1, Pallas kernels, body(): pl.pallas_call(functools.partial(kernel, steps, peers, HEADS * DH), out_s...  47.3 us
    pallas_call x1, Pallas kernels, body(): pl.pallas_call(write_out, out_shape=(big,) * 4, in_specs=[pl.BlockSpec(me...  3.37 us

profile of v2, /device:TPU:0, one launch (start us, length us, event | category | flops | bytes accessed | tf_op | source)
XLA Modules:
  0.0 51.3 jit_solution(6350859598268776150)
XLA Ops:
  0.6 47.3 %shard_map.102 = (bf16[1024,1024]{1,0:T(8,128)(2,1)S(1)}, bf16[1024,1024]{1,0:T(8,128)(2,1)S(1)}, bf16[1024,1024]{1,0:T(8,128)(2,1)S(1)}, bf16[1024,1024]{1,0:T(8,128)(2,1)S(1)}) custom-call(bf16[1024,1024]{1,0:T(8,128)(2,1)} %q_hbm.1, bf16[1024,1024]{1,0:T(8,128)(2,1)} %k_hbm.1, bf16[1024,1024]{1,0:T(8,128)(2,1)} %v_hbm.1, bf16[1024,1024]{1,0:T(8,128)(2,1)} %g_hbm.1, ...), custom_call_target="tpu_custom_call" | custom-call | tf_op jit(solution)/shard_map/pallas_call | solution.py:333
  48.0 3.4 %shard_map.103 = (bf16[1024,1024]{1,0:T(8,128)(2,1)}, bf16[1024,1024]{1,0:T(8,128)(2,1)}, bf16[1024,1024]{1,0:T(8,128)(2,1)}, bf16[1024,1024]{1,0:T(8,128)(2,1)}) custom-call(bf16[1024,1024]{1,0:T(8,128)(2,1)S(1)} %get-tuple-element.8.refs_0_, bf16[1024,1024]{1,0:T(8,128)(2,1)S(1)} %get-tuple-element.9.refs_1_, ...), custom_call_target="tpu_custom_call" | custom-call | tf_op jit(solution)/shard_map/pallas_call | solution.py:370
